TPU v7x, 32 devices: a whole 2x2x4 slice. The times are simulated.
32 devices in a mesh: gx: 8 (over z, y), gy: 4 (over x, core).
Axes of the slice: x: 2, y: 2, z: 4, core: 2. Of those that a mesh axis runs over, the one named last changes fastest.
Arguments:
- positions: float32 [3, 64, 32, 128], P(None, 'gx', 'gy'), may hold values from 0 to 12
- charges: float32 [64, 32, 128], P('gx', 'gy'), may hold values from -4 to 4
- cell_index: int32 [64, 32, 128], P('gx', 'gy'), may hold values from 0 to 32767, as said below
- task_patch: int32 [8, 4, 32], P('gx', 'gy'), may hold values from 0 to 63
- task_near: int32 [8, 4, 32], P('gx', 'gy'), may hold values from 0 to 8
- task_count: int32 [8, 4], P('gx', 'gy'), may hold values from 1 to 32, as said below
Outputs:
- forces: float32 [3, 64, 32, 128], P(None, 'gx', 'gy')
- recip_potential: float32 [64, 32, 128], P('gx', 'gy')
Inputs may be any that keep to these rules, and one draw needn't show every extreme that they name: `task_near`: code k names the neighbouring patch at offset (k // 3 - 1, k % 3 - 1) along the two patch dimensions; only slots below task_count are read. `task_patch`: only slots below task_count are read. `task_count`: in each gx row one device has 32 live tasks, and the counts of the devices that share a gx index sum to at most 4 * 16. Each atom lies in the cell that cell_index names: for an atom of local patch row r and column s with coordinates (a, b, e), the cell has z = floor(e * 256 / 12), x = (r * 4 + floor(a * 4 / 12)) // 8, y = (s * 32 + floor(b * 32 / 12)) // 8, and c = (z * 4 + x) * 32 + y.
All inputs are finite; a program needn't handle non-finite values.
Results may differ from a plain program's by a relative error of at most 0.0003.
Values sent between devices are 32-bit elements; how exact they have to be, the bound alone decides.
No kernel may reach another device: no remote copies, remote signals or barrier semaphores. Data moves between devices by JAX's collectives and lax.ppermute only.
A program may use at most 64 MiB of HBM per device.

v0:
```python
import math

import jax
import jax.numpy as jnp
import numpy as np
from jax import lax
from jax.experimental import pallas as pl
from jax.experimental.pallas import tpu as pltpu
from jax.sharding import PartitionSpec as P

XR = 4
YC = 32
GZ = 256

SCREEN = 72.0
PATCH_SIDE = 12.0
KERNEL_SCALE = 64.0
SUBLANES = 8
BOTH = ("gx", "gy")
SCRATCH = pltpu.CompilerParams(vmem_limit_bytes=16 << 20)


def from_both_sides(first, last, axis):
    count = lax.axis_size(axis)
    up = [(i, (i + 1) % count) for i in range(count)]
    down = [(j, i) for i, j in up]
    return lax.ppermute(last, axis, up), lax.ppermute(first, axis, down)


def halo_edges(positions, charges):
    atoms = [*positions, charges]
    cols = charges.shape[1]
    west, east = from_both_sides(
        jnp.stack([v[:, 0] for v in atoms]),
        jnp.stack([v[:, cols - 1] for v in atoms]),
        "gy",
    )

    def row(r):
        middle = jnp.stack([v[r] for v in atoms])
        return jnp.concatenate([west[:, r : r + 1], middle, east[:, r : r + 1]], axis=1)

    north, south = from_both_sides(row(0), row(charges.shape[0] - 1), "gx")
    return west, east, north, south


def cas_numpy(length):
    steps = np.arange(length)
    angle = (2.0 * math.pi / length) * ((steps[:, None] * steps[None, :]) % length)
    return np.cos(angle) + np.sin(angle)


def two_parts(table):
    table = np.asarray(table, np.float32)
    high = table.astype(jnp.bfloat16)
    low = (table - high.astype(np.float32)).astype(jnp.bfloat16)
    return high, low


def split(value):
    high = value.astype(jnp.bfloat16)
    low = (value - high.astype(jnp.float32)).astype(jnp.bfloat16)
    return high, low


def mm(left, right):
    return jnp.dot(left, right, preferred_element_type=jnp.float32)


def mm_lanes(left, right):
    return lax.dot_general(
        left, right, (((1,), (1,)), ((), ())), preferred_element_type=jnp.float32
    )


def force_kernel(
    patch_ref, near_ref, count_ref, pos_ref, charge_ref, west_ref, east_ref,
    north_ref, south_ref, out_ref, halo_ref,
):
    rows, cols, lanes = charge_ref.shape
    out_ref[...] = jnp.zeros_like(out_ref)
    for c in range(4):
        for r in range(rows):
            own = charge_ref[r] if c == 3 else pos_ref[c, r]
            halo_ref[c, r + 1, 1 : cols + 1, :] = own
            halo_ref[c, r + 1, 0:1, :] = west_ref[c, r : r + 1, :]
            halo_ref[c, r + 1, cols + 1 : cols + 2, :] = east_ref[c, r : r + 1, :]
        halo_ref[c, 0, : cols + 2, :] = north_ref[c]
        halo_ref[c, rows + 1, : cols + 2, :] = south_ref[c]

    def task(t, carry):
        patch = patch_ref[t]
        near = near_ref[t]
        row, col = lax.div(patch, jnp.int32(cols)), lax.rem(patch, jnp.int32(cols))
        drow = lax.div(near, jnp.int32(3)) - 1
        dcol = lax.rem(near, jnp.int32(3)) - 1

        def spot(c, r, s):
            return halo_ref[c, r, pl.ds(s, SUBLANES, stride=0), :]

        first = [spot(c, row + 1, col + 1) for c in range(4)]
        second = [spot(c, row + 1 + drow, col + 1 + dcol) for c in range(4)]
        second[0] = second[0] + drow.astype(jnp.float32) * PATCH_SIDE
        second[1] = second[1] + dcol.astype(jnp.float32) * PATCH_SIDE
        base = [pltpu.roll(v, 0, 1, stride=1, stride_axis=0) for v in second]
        sums = [jnp.zeros((SUBLANES, lanes), jnp.float32) for _ in range(3)]
        for j in range(lanes // SUBLANES):
            other = base if j == 0 else [pltpu.roll(v, j * SUBLANES, 1) for v in base]
            delta = [first[c] - other[c] for c in range(3)]
            dist_sq = delta[0] * delta[0] + delta[1] * delta[1] + delta[2] * delta[2]
            root = lax.rsqrt(dist_sq + 1.0)
            weight = other[3] * jnp.exp(dist_sq * (-1.0 / SCREEN)) * (root * root * root)
            sums = [sums[c] + weight * delta[c] for c in range(3)]
        for c in range(3):
            total = jnp.sum(sums[c], axis=0, keepdims=True) * first[3][:1]
            out_ref[c, row, pl.ds(col, 1), :] = out_ref[c, row, pl.ds(col, 1), :] + total
        return carry

    lax.fori_loop(0, count_ref[0], task, 0)


def pair_forces(positions, charges, patch, near, count):
    rows, cols, atoms = charges.shape
    edges = halo_edges(positions, charges)
    smem = pl.BlockSpec(memory_space=pltpu.SMEM)
    vmem = pl.BlockSpec(memory_space=pltpu.VMEM)
    wide = -(-(cols + 2) // SUBLANES) * SUBLANES + SUBLANES
    return pl.pallas_call(
        force_kernel,
        out_shape=jax.ShapeDtypeStruct(positions.shape, jnp.float32),
        in_specs=[smem] * 3 + [vmem] * 6,
        out_specs=vmem,
        scratch_shapes=[pltpu.VMEM((4, rows + 2, wide, atoms), jnp.float32)],
        compiler_params=SCRATCH,
        name="pair_forces",
    )(patch, near, count, positions, charges, *edges)


def cell_parts(cells, block_cells):
    plane = lax.div(cells, jnp.int32(block_cells))
    return plane, cells - plane * block_cells


def strips(rows, cols):
    deep = rows // XR
    wide = SUBLANES // (YC // cols)
    for strip in range(XR * YC // SUBLANES):
        x, part = divmod(strip, YC // SUBLANES)
        yield strip, [
            (x * deep + a, part * wide + b) for a in range(deep) for b in range(wide)
        ]


def strayed(flat, rows, cols):
    deep = rows // XR
    wide = SUBLANES // (YC // cols)
    row = lax.broadcasted_iota(jnp.int32, flat.shape, 0)
    col = lax.broadcasted_iota(jnp.int32, flat.shape, 1)
    own = lax.div(row, jnp.int32(deep)) * (YC // SUBLANES) + lax.div(col, jnp.int32(wide))
    return jnp.max((lax.div(flat, jnp.int32(SUBLANES)) != own).astype(jnp.int32))


def gather_lanes(value, places):
    return jnp.concatenate([value[r, s : s + 1, :] for r, s in places], axis=1)


def onehot_rows(index, count):
    shape = (count, index.shape[1])
    return (lax.broadcasted_iota(jnp.int32, shape, 0) == index).astype(jnp.bfloat16)


def charge_rows(index, charge, count):
    shape = (count, index.shape[1])
    here = lax.broadcasted_iota(jnp.int32, shape, 0) == index
    high, low = split(jnp.where(here, charge, 0.0))
    return jnp.concatenate([high, low], axis=0)


def spread_kernel(
    charge_hbm, cell_hbm, cas_hbm, out_ref, charge_ref, cell_ref, cas_ref, grid_ref, flat_ref,
    plane_ref, sems,
):
    loads = [
        pltpu.make_async_copy(source, target, sems.at[k])
        for k, (source, target) in enumerate(
            ((charge_hbm, charge_ref), (cell_hbm, cell_ref), (cas_hbm, cas_ref))
        )
    ]
    for load in loads:
        load.start()
    loads[0].wait()
    loads[1].wait()
    rows, cols, _ = charge_ref.shape
    block = out_ref.shape[1]
    depth = out_ref.shape[0]
    charge = charge_ref[...]
    plane, flat = cell_parts(cell_ref[...], block)
    for strip, places in strips(rows, cols):
        index = gather_lanes(flat, places) - strip * SUBLANES
        lines = charge_rows(index, gather_lanes(charge, places), SUBLANES)
        both = mm_lanes(lines, onehot_rows(gather_lanes(plane, places), depth))
        grid_ref[strip * SUBLANES : (strip + 1) * SUBLANES, :] = (
            both[:SUBLANES] + both[SUBLANES:]
        )

    @pl.when(strayed(flat, rows, cols) > 0)
    def _():
        plane_ref[...] = plane.reshape(plane_ref.shape)
        flat_ref[...] = flat.reshape(flat_ref.shape)
        grid_ref[...] = jnp.zeros_like(grid_ref)

        def patch(p, carry):
            row, col = lax.div(p, jnp.int32(cols)), lax.rem(p, jnp.int32(cols))
            lines = charge_rows(
                flat_ref[pl.ds(p, 1), :], charge_ref[row, pl.ds(col, 1), :], block
            )
            both = mm_lanes(lines, onehot_rows(plane_ref[pl.ds(p, 1), :], depth))
            grid_ref[...] = grid_ref[...] + both[:block] + both[block:]
            return carry

        lax.fori_loop(0, rows * cols, patch, 0)

    loads[2].wait()
    high, low = split(grid_ref[...])
    twice = mm_lanes(cas_ref[...], high)
    out_ref[...] = twice[:depth] + twice[depth:] + mm_lanes(cas_ref[:depth], low)


def spread_planes(charges, cells, cas_z):
    rows, cols, atoms = charges.shape
    return pl.pallas_call(
        spread_kernel,
        out_shape=pltpu.VMEM((GZ, XR * YC), jnp.float32),
        in_specs=[pl.BlockSpec(memory_space=pltpu.HBM)] * 3,
        out_specs=pl.BlockSpec(memory_space=pltpu.VMEM),
        scratch_shapes=[
            pltpu.VMEM(charges.shape, charges.dtype),
            pltpu.VMEM(cells.shape, cells.dtype),
            pltpu.VMEM(cas_z.shape, cas_z.dtype),
            pltpu.VMEM((XR * YC, GZ), jnp.float32),
            pltpu.VMEM((rows * cols, atoms), jnp.int32),
            pltpu.VMEM((rows * cols, atoms), jnp.int32),
            pltpu.SemaphoreType.DMA((3,)),
        ],
        compiler_params=SCRATCH,
        name="spread",
    )(*(pltpu.with_memory_space_constraint(v, pltpu.HBM) for v in (charges, cells, cas_z)))


def sample_kernel(planes_ref, cell_ref, cas_ref, out_ref, field_ref, flat_ref, plane_ref):
    rows, cols, _ = cell_ref.shape
    depth, block = planes_ref.shape
    plane, flat = cell_parts(cell_ref[...], block)
    high, low = split(planes_ref[...].T)
    pair = mm(jnp.concatenate([high, low], axis=0), cas_ref[:depth])
    field = pair[:block] + pair[block:] + mm(high, cas_ref[depth:])
    field_high, field_low = split(field)
    for strip, places in strips(rows, cols):
        span = slice(strip * SUBLANES, (strip + 1) * SUBLANES)
        lines = jnp.concatenate([field_high[span], field_low[span]], axis=0)
        both = mm(lines, onehot_rows(gather_lanes(plane, places), depth))
        value = both[:SUBLANES] + both[SUBLANES:]
        index = gather_lanes(flat, places) - strip * SUBLANES
        here = lax.broadcasted_iota(jnp.int32, value.shape, 0) == index
        found = jnp.sum(jnp.where(here, value, 0.0), axis=0, keepdims=True)
        atoms = out_ref.shape[2]
        for k, (r, s) in enumerate(places):
            out_ref[r, s : s + 1, :] = found[:, k * atoms : (k + 1) * atoms]

    @pl.when(strayed(flat, rows, cols) > 0)
    def _():
        plane_ref[...] = plane.reshape(plane_ref.shape)
        flat_ref[...] = flat.reshape(flat_ref.shape)
        field_ref[:block, :] = field_high
        field_ref[block:, :] = field_low

        def patch(p, carry):
            row, col = lax.div(p, jnp.int32(cols)), lax.rem(p, jnp.int32(cols))
            both = mm(field_ref[...], onehot_rows(plane_ref[pl.ds(p, 1), :], depth))
            value = both[:block] + both[block:]
            here = lax.broadcasted_iota(jnp.int32, value.shape, 0) == flat_ref[pl.ds(p, 1), :]
            out_ref[row, pl.ds(col, 1), :] = jnp.sum(
                jnp.where(here, value, 0.0), axis=0, keepdims=True
            )
            return carry

        lax.fori_loop(0, rows * cols, patch, 0)


def sample_planes(planes, cells, cas_z):
    rows, cols, atoms = cells.shape
    vmem = pl.BlockSpec(memory_space=pltpu.VMEM)
    return pl.pallas_call(
        sample_kernel,
        out_shape=jax.ShapeDtypeStruct(cells.shape, jnp.float32),
        in_specs=[vmem] * 3,
        out_specs=vmem,
        scratch_shapes=[
            pltpu.VMEM((2 * XR * YC, GZ), jnp.bfloat16),
            pltpu.VMEM((rows * cols, atoms), jnp.int32),
            pltpu.VMEM((rows * cols, atoms), jnp.int32),
        ],
        compiler_params=SCRATCH,
        name="sample",
    )(planes, cells, cas_z)


def wave_part(freq, length):
    folded = jnp.minimum(freq, length - freq).astype(jnp.float32) / length
    return folded * folded


def influence(depth_freq, row_freq, column_freq, depth_len, row_len, column_len):
    wave_sq = (
        wave_part(depth_freq, depth_len)[:, None, None]
        + wave_part(row_freq, row_len)[None, :, None]
        + wave_part(column_freq, column_len)[None, None, :]
    )
    safe = jnp.where(wave_sq > 0, wave_sq, 1.0)
    return jnp.where(wave_sq > 0, 1.0 / (KERNEL_SCALE * safe), 0.0)


def plane_tables(n_x, n_y, share):
    total_x, total_y = n_x * XR, n_y * YC
    cas_x, cas_y = cas_numpy(total_x), cas_numpy(total_y)
    along_y = np.repeat(cas_y.reshape(n_y, 1, YC, total_y), XR, axis=1)
    along_y = along_y.reshape(n_y * XR * YC, total_y)
    to_m = cas_x.reshape(n_x, XR, total_x).transpose(2, 1, 0)
    to_m = np.einsum("mxi,ab->maxib", to_m, np.eye(share))
    to_m = to_m.reshape(total_x * share, XR * n_x * share)
    y_high, y_low = two_parts(along_y)
    x_high, x_low = two_parts(to_m)
    return (
        np.concatenate([y_high, y_low], axis=1),
        np.concatenate([x_high, x_low], axis=0),
        np.concatenate([x_high.T, x_low.T], axis=0),
        np.concatenate([y_high.T, y_high.T, y_low.T], axis=0),
    )


def xy_kernel(planes_ref, scale_ref, y_ref, x_ref, back_x_ref, back_y_ref, out_ref, *, n_x, n_y):
    _, share, block = planes_ref.shape
    total_y = n_y * YC
    lanes = n_y * block
    blocks = planes_ref[...].reshape(n_x, n_y, share, block)
    lines = jnp.concatenate(
        [blocks[:, j].reshape(n_x * share, block) for j in range(n_y)], axis=1
    )
    owner = lax.div(
        lax.rem(lax.broadcasted_iota(jnp.int32, (n_x * share, lanes), 1), jnp.int32(block)),
        jnp.int32(YC),
    )
    stacked = jnp.concatenate([jnp.where(owner == x, lines, 0.0) for x in range(XR)], axis=0)
    high, low = split(stacked)
    pair = mm(high, y_ref[...])
    along_y = pair[:, :total_y] + pair[:, total_y:] + mm(low, y_ref[:, :total_y])

    def along_x(value, table_ref):
        count = table_ref.shape[0] // 2
        both = mm(table_ref[...], jnp.concatenate(split(value), axis=1))
        return both[:count, :total_y] + both[:count, total_y:] + both[count:, :total_y]

    solved = along_x(along_x(along_y, x_ref) * scale_ref[...], back_x_ref)
    high, low = split(solved)
    wide = mm(jnp.concatenate([high, low, high], axis=1), back_y_ref[...])
    span = n_x * share
    lines = wide[:span]
    for x in range(1, XR):
        lines = jnp.where(owner == x, wide[x * span : (x + 1) * span], lines)
    for i in range(n_x):
        for j in range(n_y):
            out_ref[i * n_y + j] = lines[i * share : (i + 1) * share, j * block : (j + 1) * block]


def solve_planes(planes):
    n_x, n_y = lax.axis_size("gx"), lax.axis_size("gy")
    share = planes.shape[0] // (n_x * n_y)
    block = planes.shape[1]
    total_x, total_y = n_x * XR, n_y * YC
    first = (lax.axis_index("gx") * n_y + lax.axis_index("gy")) * share
    scale = influence(
        first + jnp.arange(share, dtype=jnp.int32),
        jnp.arange(total_x, dtype=jnp.int32),
        jnp.arange(total_y, dtype=jnp.int32),
        GZ,
        total_x,
        total_y,
    ) / (total_x * total_y * GZ)
    scale = jnp.swapaxes(scale, 0, 1).reshape(total_x * share, total_y)
    held = planes.reshape(n_x * n_y, share, block)
    held = lax.all_to_all(held, BOTH, split_axis=0, concat_axis=0, tiled=True)
    vmem = pl.BlockSpec(memory_space=pltpu.VMEM)
    held = pl.pallas_call(
        lambda *refs: xy_kernel(*refs, n_x=n_x, n_y=n_y),
        out_shape=pltpu.VMEM(held.shape, jnp.float32),
        in_specs=[vmem] * 6,
        out_specs=vmem,
        compiler_params=SCRATCH,
        name="xy_solve",
    )(held, scale, *(jnp.asarray(t) for t in plane_tables(n_x, n_y, share)))
    held = lax.all_to_all(held, BOTH, split_axis=0, concat_axis=0, tiled=True)
    return held.reshape(planes.shape)


def cas_table(length):
    return jnp.asarray(cas_numpy(length).astype(np.float32))


def solve_pencils(planes):
    high = lax.Precision.HIGHEST
    ztrans = planes.reshape(GZ, XR, YC)
    turned = lax.all_to_all(ztrans, "gy", split_axis=0, concat_axis=2, tiled=True)
    total_y = turned.shape[2]
    ytrans = jnp.einsum("zxy,yk->zxk", turned, cas_table(total_y), precision=high)
    turned = lax.all_to_all(ytrans, "gx", split_axis=2, concat_axis=1, tiled=True)
    depth_share, total_x, width_share = turned.shape
    cas_x = cas_table(total_x)
    xtrans = jnp.einsum("zxy,xm->zmy", turned, cas_x, precision=high)
    depth_freq = lax.axis_index("gy") * depth_share + jnp.arange(depth_share, dtype=jnp.int32)
    column_freq = lax.axis_index("gx") * width_share + jnp.arange(width_share, dtype=jnp.int32)
    scale = influence(
        depth_freq, jnp.arange(total_x, dtype=jnp.int32), column_freq, GZ, total_x, total_y
    ) / (total_x * total_y * GZ)
    xback = jnp.einsum("zmy,mx->zxy", xtrans * scale, cas_x, precision=high)
    rows_back = lax.all_to_all(xback, "gx", split_axis=1, concat_axis=2, tiled=True)
    yback = jnp.einsum("zxk,ky->zxy", rows_back, cas_table(total_y), precision=high)
    planes_back = lax.all_to_all(yback, "gy", split_axis=2, concat_axis=0, tiled=True)
    return planes_back.reshape(planes.shape)


def whole_planes(devices):
    return GZ % (devices * SUBLANES) == 0


def body(positions, charges, cell_index, task_patch, task_near, task_count):
    cas_z = jnp.asarray(np.concatenate(two_parts(cas_numpy(GZ)), axis=0))
    planes = spread_planes(charges, cell_index, cas_z)
    devices = lax.axis_size("gx") * lax.axis_size("gy")
    planes = (solve_planes if whole_planes(devices) else solve_pencils)(planes)
    recip_potential = sample_planes(planes, cell_index, cas_z)
    forces = pair_forces(
        positions,
        charges,
        task_patch.reshape(-1),
        task_near.reshape(-1),
        task_count.reshape(-1),
    )
    return (forces, recip_potential)


def solution(mesh):
    return jax.shard_map(
        body,
        mesh=mesh,
        in_specs=(
            P(None, "gx", "gy", None),
            P("gx", "gy", None),
            P("gx", "gy", None),
            P("gx", "gy", None),
            P("gx", "gy", None),
            P("gx", "gy"),
        ),
        out_specs=(P(None, "gx", "gy", None), P("gx", "gy", None)),
        check_vma=False,
    )
```

profile of v0, /device:TPU:3, one launch (start us, length us, event | category | flops | bytes accessed | tf_op | source)
XLA Modules:
  0.0 43.9 jit_solution(1392885081730305839)
XLA Ops:
  0.6 0.8 %fusion.15 = (f32[8,1,128]{2,1,0:T(1,128)S(1)}, f32[8,1,128]{2,1,0:T(1,128)S(1)}) fusion(f32[8,8,128]{2,1,0:T(8,128)} %charge_hbm.1), kind=kLoop, calls=%fused_computation.40 | loop fusion | bytes 16384 | tf_op jit(solution)/shard_map/slice | solution.py:34
  1.5 0.8 %fusion.13 = (f32[1,8,8,128]{3,2,1,0:T(8,128)S(1)}, f32[1,8,8,128]{3,2,1,0:T(8,128)S(1)}, f32[1,8,8,128]{3,2,1,0:T(8,128)S(1)}) fusion(f32[3,8,8,128]{3,2,1,0:T(8,128)} %pos_ref.1), kind=kLoop, calls=%fused_computation.38 | loop fusion | bytes 196608 | tf_op jit(solution)/shard_map/unstack | solution.py:31
  2.3 0.0 copy-start.6
  2.4 0.1 collective-permute-start
  2.4 0.0 copy-start.4
  2.5 0.0 copy-start.2
  2.5 0.7 %collective-permute-start.1 = (f32[4,8,128]{2,1,0:T(8,128)S(1)}, f32[4,8,128]{2,1,0:T(8,128)S(1)}, u32[]{:S(2)}, u32[]{:S(2)}) collective-permute-start(f32[4,8,128]{2,1,0:T(8,128)S(1)} %pad_maximum_fusion.3), channel_id=1, source_target_pairs={{1,0},{2,1},{3,2},{0,3},{5,4},{6,5},{7,6},{4,7},{9,8},{10,9},{11,1... | collective-permute-start | bytes 49160 | tf_op jit(solution)/shard_map/ppermute | solution.py:27
  3.2 2.9 %spread.1 = f32[256,128]{1,0:T(8,128)} custom-call(f32[8,8,128]{2,1,0:T(8,128)} %charge_hbm.1, s32[8,8,128]{2,1,0:T(8,128)} %cell_ref.1, bf16[512,256]{1,0:T(8,128)(2,1)} %constant.49.clone.cas_hbm.cas_ref), custom_call_target="tpu_custom_call" | custom-call | tf_op jit(solution)/shard_map/spread/pallas_call | solution.py:231
  6.1 0.0 copy-start.1
  6.1 0.0 copy-start.3
  6.2 7.4 %all-to-all-start = ((f32[32,8,128]{2,1,0:T(8,128)}), f32[32,8,128]{2,1,0:T(8,128)S(1)}, u32[]{:S(2)}, u32[]{:S(2)}) async-start(f32[32,8,128]{2,1,0:T(8,128)} %bitcast.20), calls=%async_computation | async-start | bytes 262144 | tf_op jit(solution)/shard_map/all_to_all | solution.py:391
  13.6 0.0 copy-done.1
  13.7 0.1 broadcast_add_fusion
  13.8 0.1 add.57
  13.8 0.1 fusion.1.refs_1_
  14.0 0.0 copy-done.6
  14.0 0.0 collective-permute-done.1.east_ref
  14.0 6.5 %all-to-all-done.refs_0_ = f32[32,8,128]{2,1,0:T(8,128)S(1)} async-done(((f32[32,8,128]{2,1,0:T(8,128)}), f32[32,8,128]{2,1,0:T(8,128)S(1)}, u32[]{:S(2)}, u32[]{:S(2)}) %all-to-all-start) | async-done | bytes 131104 | tf_op jit(solution)/shard_map/all_to_all | solution.py:391
  20.5 0.0 copy-done.5
  20.5 0.0 copy-done.2
  20.5 1.7 %xy_solve.1 = f32[32,8,128]{2,1,0:T(8,128)} custom-call(f32[32,8,128]{2,1,0:T(8,128)S(1)} %all-to-all-done.refs_0_, f32[256,128]{1,0:T(8,128)S(1)} %fusion.1.refs_1_, bf16[512,256]{1,0:T(8,128)(2,1)S(1)} %copy-done.3, bf16[512,256]{1,0:T(8,128)(2,1)S(1)} %copy-done.4, bf16[512,256]{1,0:T(8,128)(2,1)S(1)} %copy-done.5, bf16[384,512]{1,0:T(8,128)(2,1)S(1)} %copy-done.2), custom_call_target="tpu_custom_call" | custom-call | tf_op jit(solution)/shard_map/xy_solve/pallas_call | solution.py:393
  22.2 3.9 %all-to-all-start.1 = ((f32[32,8,128]{2,1,0:T(8,128)}), f32[32,8,128]{2,1,0:T(8,128)S(1)}, u32[]{:S(2)}, u32[]{:S(2)}) async-start(f32[32,8,128]{2,1,0:T(8,128)} %xy_solve.1), calls=%async_computation.1 | async-start | bytes 262144 | tf_op jit(solution)/shard_map/all_to_all | solution.py:401
  26.1 0.0 copy-start
  26.1 0.0 collective-permute-done.west_ref
  26.2 1.3 %collective-permute-start.2 = (f32[4,10,128]{2,1,0:T(8,128)S(1)}, f32[4,10,128]{2,1,0:T(8,128)S(1)}, u32[]{:S(2)}, u32[]{:S(2)}) collective-permute-start(f32[4,10,128]{2,1,0:T(8,128)S(1)} %pad_maximum_fusion), channel_id=1, source_target_pairs={{0,4},{4,8},{8,12},{12,16},{16,20},{20,24},{24,28},{28,0},{1,5},{5... | collective-permute-start | bytes 61448 | tf_op jit(solution)/shard_map/ppermute | solution.py:27
  27.5 3.0 %collective-permute-start.3 = (f32[4,10,128]{2,1,0:T(8,128)S(1)}, f32[4,10,128]{2,1,0:T(8,128)S(1)}, u32[]{:S(2)}, u32[]{:S(2)}) collective-permute-start(f32[4,10,128]{2,1,0:T(8,128)S(1)} %pad_maximum_fusion.1), channel_id=1, source_target_pairs={{4,0},{8,4},{12,8},{16,12},{20,16},{24,20},{28,24},{0,28},{5,1},{9... | collective-permute-start | bytes 61448 | tf_op jit(solution)/shard_map/ppermute | solution.py:27
  31.1 2.4 %collective-permute-done.2.north_ref = f32[4,10,128]{2,1,0:T(8,128)S(1)} collective-permute-done((f32[4,10,128]{2,1,0:T(8,128)S(1)}, f32[4,10,128]{2,1,0:T(8,128)S(1)}, u32[]{:S(2)}, u32[]{:S(2)}) %collective-permute-start.2) | collective-permute-done | bytes 20512 | tf_op jit(solution)/shard_map/ppermute | solution.py:27
  33.5 0.0 collective-permute-done.3.south_ref
  33.5 0.0 copy-start.7
  33.5 8.7 %pair_forces.1 = f32[3,8,8,128]{3,2,1,0:T(8,128)} custom-call(s32[32]{0:T(128)S(1)} %bitcast.44, s32[32]{0:T(128)S(1)} %bitcast.45, s32[1]{0:T(128)} %bitcast.42.count_ref, f32[3,8,8,128]{3,2,1,0:T(8,128)S(1)} %copy-done.1, f32[8,8,128]{2,1,0:T(8,128)S(1)} %copy-done.6, f32[4,8,128]{2,1,0:T(8,128)S(1)} %collective-permute-done.west_ref, ...), custom_call_target="tpu_custom_call" | custom-call | tf_op jit(solution)/shard_map/pair_forces/pallas_call | solution.py:128
  42.2 0.0 all-to-all-done.1
  42.2 1.7 %sample.1 = f32[8,8,128]{2,1,0:T(8,128)} custom-call(f32[256,128]{1,0:T(8,128)S(1)} %bitcast.43, s32[8,8,128]{2,1,0:T(8,128)S(1)} %copy-done.7, bf16[512,256]{1,0:T(8,128)(2,1)S(1)} %copy-done), custom_call_target="tpu_custom_call" | custom-call | tf_op jit(solution)/shard_map/sample/pallas_call | solution.py:293
  (25 shorter events, 0.1 us)
Async XLA Ops:
  2.3 18.2 %copy-start.5 = (bf16[512,256]{1,0:T(8,128)(2,1)S(1)}, bf16[512,256]{1,0:T(8,128)(2,1)}, u32[]{:S(2)}) copy-start(bf16[512,256]{1,0:T(8,128)(2,1)} %constant.52.clone.refs_4_) | copy-start | bytes 786436
  2.3 11.6 %copy-start.6 = (f32[8,8,128]{2,1,0:T(8,128)S(1)}, f32[8,8,128]{2,1,0:T(8,128)}, u32[]{:S(2)}) copy-start(f32[8,8,128]{2,1,0:T(8,128)} %charge_hbm.1) | copy-start | bytes 98308
  2.4 23.8 %collective-permute-start = (f32[4,8,128]{2,1,0:T(8,128)S(1)}, f32[4,8,128]{2,1,0:T(8,128)S(1)}, u32[]{:S(2)}, u32[]{:S(2)}) collective-permute-start(f32[4,8,128]{2,1,0:T(8,128)S(1)} %pad_maximum_fusion.2), channel_id=1, source_target_pairs={{0,1},{1,2},{2,3},{3,0},{4,5},{5,6},{6,7},{7,4},{8,9},{9,10},{10,1... | collective-permute-start | bytes 49160 | tf_op jit(solution)/shard_map/ppermute | solution.py:27
  2.4 18.1 %copy-start.4 = (bf16[512,256]{1,0:T(8,128)(2,1)S(1)}, bf16[512,256]{1,0:T(8,128)(2,1)}, u32[]{:S(2)}) copy-start(bf16[512,256]{1,0:T(8,128)(2,1)} %constant.51.clone.refs_3_) | copy-start | bytes 786436
  2.5 18.0 %copy-start.2 = (bf16[384,512]{1,0:T(8,128)(2,1)S(1)}, bf16[384,512]{1,0:T(8,128)(2,1)}, u32[]{:S(2)}) copy-start(bf16[384,512]{1,0:T(8,128)(2,1)} %constant.53.clone.refs_5_) | copy-start | bytes 1179652
  2.5 11.5 %collective-permute-start.1 = (f32[4,8,128]{2,1,0:T(8,128)S(1)}, f32[4,8,128]{2,1,0:T(8,128)S(1)}, u32[]{:S(2)}, u32[]{:S(2)}) collective-permute-start(f32[4,8,128]{2,1,0:T(8,128)S(1)} %pad_maximum_fusion.3), channel_id=1, source_target_pairs={{1,0},{2,1},{3,2},{0,3},{5,4},{6,5},{7,6},{4,7},{9,8},{10,9},{11,1... | collective-permute-start | bytes 49160 | tf_op jit(solution)/shard_map/ppermute | solution.py:27
  6.1 7.5 %copy-start.1 = (f32[3,8,8,128]{3,2,1,0:T(8,128)S(1)}, f32[3,8,8,128]{3,2,1,0:T(8,128)}, u32[]{:S(2)}) copy-start(f32[3,8,8,128]{3,2,1,0:T(8,128)} %pos_ref.1) | copy-start | bytes 294916
  6.1 14.4 %copy-start.3 = (bf16[512,256]{1,0:T(8,128)(2,1)S(1)}, bf16[512,256]{1,0:T(8,128)(2,1)}, u32[]{:S(2)}) copy-start(bf16[512,256]{1,0:T(8,128)(2,1)} %constant.50.clone.refs_2_) | copy-start | bytes 786436
  6.2 14.3 %all-to-all-start = ((f32[32,8,128]{2,1,0:T(8,128)}), f32[32,8,128]{2,1,0:T(8,128)S(1)}, u32[]{:S(2)}, u32[]{:S(2)}) async-start(f32[32,8,128]{2,1,0:T(8,128)} %bitcast.20), calls=%async_computation | async-start | bytes 262144 | tf_op jit(solution)/shard_map/all_to_all | solution.py:391
  22.2 11.3 %copy-start.8 = (s32[1,1,32]{2,1,0:T(1,128)S(1)}, s32[1,1,32]{2,1,0:T(1,128)}, u32[]{:S(2)}) copy-start(s32[1,1,32]{2,1,0:T(1,128)} %param.14) | copy-start | bytes 388
  22.2 11.3 %copy-start.9 = (s32[1,1,32]{2,1,0:T(1,128)S(1)}, s32[1,1,32]{2,1,0:T(1,128)}, u32[]{:S(2)}) copy-start(s32[1,1,32]{2,1,0:T(1,128)} %param.15) | copy-start | bytes 388
  22.2 20.0 %all-to-all-start.1 = ((f32[32,8,128]{2,1,0:T(8,128)}), f32[32,8,128]{2,1,0:T(8,128)S(1)}, u32[]{:S(2)}, u32[]{:S(2)}) async-start(f32[32,8,128]{2,1,0:T(8,128)} %xy_solve.1), calls=%async_computation.1 | async-start | bytes 262144 | tf_op jit(solution)/shard_map/all_to_all | solution.py:401
  26.1 16.1 %copy-start = (bf16[512,256]{1,0:T(8,128)(2,1)S(1)}, bf16[512,256]{1,0:T(8,128)(2,1)}, u32[]{:S(2)}) copy-start(bf16[512,256]{1,0:T(8,128)(2,1)} %constant.49.clone.cas_hbm.cas_ref) | copy-start | bytes 786436
  26.2 7.3 %collective-permute-start.2 = (f32[4,10,128]{2,1,0:T(8,128)S(1)}, f32[4,10,128]{2,1,0:T(8,128)S(1)}, u32[]{:S(2)}, u32[]{:S(2)}) collective-permute-start(f32[4,10,128]{2,1,0:T(8,128)S(1)} %pad_maximum_fusion), channel_id=1, source_target_pairs={{0,4},{4,8},{8,12},{12,16},{16,20},{20,24},{24,28},{28,0},{1,5},{5... | collective-permute-start | bytes 61448 | tf_op jit(solution)/shard_map/ppermute | solution.py:27
  27.5 6.1 %collective-permute-start.3 = (f32[4,10,128]{2,1,0:T(8,128)S(1)}, f32[4,10,128]{2,1,0:T(8,128)S(1)}, u32[]{:S(2)}, u32[]{:S(2)}) collective-permute-start(f32[4,10,128]{2,1,0:T(8,128)S(1)} %pad_maximum_fusion.1), channel_id=1, source_target_pairs={{4,0},{8,4},{12,8},{16,12},{20,16},{24,20},{28,24},{0,28},{5,1},{9... | collective-permute-start | bytes 61448 | tf_op jit(solution)/shard_map/ppermute | solution.py:27
  33.5 8.7 %copy-start.7 = (s32[8,8,128]{2,1,0:T(8,128)S(1)}, s32[8,8,128]{2,1,0:T(8,128)}, u32[]{:S(2)}) copy-start(s32[8,8,128]{2,1,0:T(8,128)} %cell_ref.1) | copy-start | bytes 98308
where the time goes:
time: 44.3 us; the launch traced here: 43.9 us
  starting transfers between devices  16.4 us (37%)
  Pallas kernels  15 us (34%)
  waiting for transfers between devices  8.9 us (20%)
  local copies, waits for them, and re-layouts  1.84 us (4%)
  between operations  1.56 us (4%)
    all_to_all x2, starting transfers between devices, solve_planes(): held = lax.all_to_all(held, BOTH, split_axis=0, concat_axis=0, tiled=True)  11.3 us
    pallas_call x1, Pallas kernels, pair_forces(): pl.pallas_call(force_kernel, out_shape=jax.ShapeDtypeStruct(positions.sha...  8.65 us
    all_to_all x2, waiting for transfers between devices, solve_planes(): held = lax.all_to_all(held, BOTH, split_axis=0, concat_axis=0, tiled=True)  6.48 us
    ppermute x4, starting transfers between devices, from_both_sides(): return (lax.ppermute(last, axis, up), lax.ppermute(first, axis, down))  5.05 us
    pallas_call x1, Pallas kernels, spread_planes(): pl.pallas_call(spread_kernel, out_shape=pltpu.VMEM((GZ, XR * YC), jnp.flo...  2.93 us
    ppermute x4, waiting for transfers between devices, from_both_sides(): return (lax.ppermute(last, axis, up), lax.ppermute(first, axis, down))  2.42 us
    pallas_call x1, Pallas kernels, sample_planes(): pl.pallas_call(sample_kernel, out_shape=jax.ShapeDtypeStruct(cells.shape,...  1.71 us
    pallas_call x1, Pallas kernels, solve_planes(): pl.pallas_call(lambda *refs: xy_kernel(*refs, n_x=n_x, n_y=n_y), out_shap...  1.69 us
  transfers between devices with their start and end apart: 6, of which 2 were waited for; matrix products, arithmetic and copies ran while one was open for 1% of the time, Pallas kernels for 30%

commit v1 on v0

--- a/solution.py
+++ b/solution.py
@@ -15,7 +15,11 @@
 SCREEN = 72.0
 PATCH_SIDE = 12.0
 KERNEL_SCALE = 64.0
+DECAY = -math.log2(math.e) / SCREEN
+TASKS = 2
 SUBLANES = 8
+SPREAD_CHUNK = 64
+SAMPLE_CHUNK = 128
 BOTH = ("gx", "gy")
 SCRATCH = pltpu.CompilerParams(vmem_limit_bytes=16 << 20)
 
@@ -88,35 +92,41 @@
         halo_ref[c, 0, : cols + 2, :] = north_ref[c]
         halo_ref[c, rows + 1, : cols + 2, :] = south_ref[c]
 
-    def task(t, carry):
-        patch = patch_ref[t]
-        near = near_ref[t]
+    def spot(c, r, s):
+        return halo_ref[c, r, pl.ds(s, SUBLANES, stride=0), :]
+
+    def start(t):
+        patch, near = patch_ref[0, 0, t], near_ref[0, 0, t]
         row, col = lax.div(patch, jnp.int32(cols)), lax.rem(patch, jnp.int32(cols))
         drow = lax.div(near, jnp.int32(3)) - 1
         dcol = lax.rem(near, jnp.int32(3)) - 1
-
-        def spot(c, r, s):
-            return halo_ref[c, r, pl.ds(s, SUBLANES, stride=0), :]
-
         first = [spot(c, row + 1, col + 1) for c in range(4)]
         second = [spot(c, row + 1 + drow, col + 1 + dcol) for c in range(4)]
         second[0] = second[0] + drow.astype(jnp.float32) * PATCH_SIDE
         second[1] = second[1] + dcol.astype(jnp.float32) * PATCH_SIDE
-        base = [pltpu.roll(v, 0, 1, stride=1, stride_axis=0) for v in second]
-        sums = [jnp.zeros((SUBLANES, lanes), jnp.float32) for _ in range(3)]
+        return row, col, first, [pltpu.roll(v, 0, 1, stride=1, stride_axis=0) for v in second]
+
+    def pair(p, carry):
+        last = count_ref[0, 0] - 1
+        times = [p * TASKS + k for k in range(TASKS)]
+        tasks = [start(jnp.minimum(t, last)) for t in times]
+        sums = [[jnp.zeros((SUBLANES, lanes), jnp.float32)] * 3 for _ in tasks]
         for j in range(lanes // SUBLANES):
-            other = base if j == 0 else [pltpu.roll(v, j * SUBLANES, 1) for v in base]
-            delta = [first[c] - other[c] for c in range(3)]
-            dist_sq = delta[0] * delta[0] + delta[1] * delta[1] + delta[2] * delta[2]
-            root = lax.rsqrt(dist_sq + 1.0)
-            weight = other[3] * jnp.exp(dist_sq * (-1.0 / SCREEN)) * (root * root * root)
-            sums = [sums[c] + weight * delta[c] for c in range(3)]
-        for c in range(3):
-            total = jnp.sum(sums[c], axis=0, keepdims=True) * first[3][:1]
-            out_ref[c, row, pl.ds(col, 1), :] = out_ref[c, row, pl.ds(col, 1), :] + total
+            for k, (_, _, first, base) in enumerate(tasks):
+                other = base if j == 0 else [pltpu.roll(v, j * SUBLANES, 1) for v in base]
+                delta = [first[c] - other[c] for c in range(3)]
+                dist_sq = delta[0] * delta[0] + delta[1] * delta[1] + delta[2] * delta[2]
+                root = lax.rsqrt(dist_sq + 1.0)
+                weight = other[3] * jnp.exp2(dist_sq * DECAY) * (root * root * root)
+                sums[k] = [sums[k][c] + weight * delta[c] for c in range(3)]
+        for t, (row, col, first, _), total in zip(times, tasks, sums):
+            scale = first[3][:1] * (t <= last).astype(jnp.float32)
+            for c in range(3):
+                found = jnp.sum(total[c], axis=0, keepdims=True) * scale
+                out_ref[c, row, pl.ds(col, 1), :] = out_ref[c, row, pl.ds(col, 1), :] + found
         return carry
 
-    lax.fori_loop(0, count_ref[0], task, 0)
+    lax.fori_loop(0, lax.div(count_ref[0, 0] + (TASKS - 1), jnp.int32(TASKS)), pair, 0)
 
 
 def pair_forces(positions, charges, patch, near, count):
@@ -164,16 +174,27 @@
     return jnp.concatenate([value[r, s : s + 1, :] for r, s in places], axis=1)
 
 
+def as_level(index):
+    return index.astype(jnp.float32).astype(jnp.bfloat16)
+
+
+def matches(index, count):
+    shape = (count, index.shape[1])
+    level = as_level(lax.broadcasted_iota(jnp.int32, (count, 128), 0))
+    level = jnp.concatenate([level] * (shape[1] // 128), axis=1)
+    return level == jnp.broadcast_to(as_level(index), shape)
+
+
 def onehot_rows(index, count):
-    shape = (count, index.shape[1])
-    return (lax.broadcasted_iota(jnp.int32, shape, 0) == index).astype(jnp.bfloat16)
+    return jnp.where(matches(index, count), jnp.bfloat16(1), jnp.bfloat16(0))
 
 
 def charge_rows(index, charge, count):
-    shape = (count, index.shape[1])
-    here = lax.broadcasted_iota(jnp.int32, shape, 0) == index
-    high, low = split(jnp.where(here, charge, 0.0))
-    return jnp.concatenate([high, low], axis=0)
+    here = matches(index, count)
+    return jnp.concatenate(
+        [jnp.where(here, jnp.broadcast_to(v, here.shape), jnp.bfloat16(0)) for v in split(charge)],
+        axis=0,
+    )
 
 
 def spread_kernel(
@@ -195,12 +216,16 @@
     depth = out_ref.shape[0]
     charge = charge_ref[...]
     plane, flat = cell_parts(cell_ref[...], block)
+    outer, inner = cell_parts(plane, SPREAD_CHUNK)
+    chunk = outer * SUBLANES
+    tall = depth // SPREAD_CHUNK * SUBLANES
     for strip, places in strips(rows, cols):
-        index = gather_lanes(flat, places) - strip * SUBLANES
-        lines = charge_rows(index, gather_lanes(charge, places), SUBLANES)
-        both = mm_lanes(lines, onehot_rows(gather_lanes(plane, places), depth))
-        grid_ref[strip * SUBLANES : (strip + 1) * SUBLANES, :] = (
-            both[:SUBLANES] + both[SUBLANES:]
+        index = gather_lanes(chunk + flat, places) - strip * SUBLANES
+        lines = charge_rows(index, gather_lanes(charge, places), tall)
+        both = mm_lanes(lines, onehot_rows(gather_lanes(inner, places), SPREAD_CHUNK))
+        both = both[:tall] + both[tall:]
+        grid_ref[strip * SUBLANES : (strip + 1) * SUBLANES, :] = jnp.concatenate(
+            [both[k : k + SUBLANES] for k in range(0, tall, SUBLANES)], axis=1
         )
 
     @pl.when(strayed(flat, rows, cols) > 0)
@@ -254,13 +279,18 @@
     high, low = split(planes_ref[...].T)
     pair = mm(jnp.concatenate([high, low], axis=0), cas_ref[:depth])
     field = pair[:block] + pair[block:] + mm(high, cas_ref[depth:])
-    field_high, field_low = split(field)
+    outer, inner = cell_parts(plane, SAMPLE_CHUNK)
+    chunk = outer * SUBLANES
+    tall = depth // SAMPLE_CHUNK * SUBLANES
     for strip, places in strips(rows, cols):
-        span = slice(strip * SUBLANES, (strip + 1) * SUBLANES)
-        lines = jnp.concatenate([field_high[span], field_low[span]], axis=0)
-        both = mm(lines, onehot_rows(gather_lanes(plane, places), depth))
-        value = both[:SUBLANES] + both[SUBLANES:]
-        index = gather_lanes(flat, places) - strip * SUBLANES
+        lines = field[strip * SUBLANES : (strip + 1) * SUBLANES]
+        lines = jnp.concatenate(
+            [lines[:, k : k + SAMPLE_CHUNK] for k in range(0, depth, SAMPLE_CHUNK)], axis=0
+        )
+        lines = jnp.concatenate(split(lines), axis=0)
+        both = mm(lines, onehot_rows(gather_lanes(inner, places), SAMPLE_CHUNK))
+        value = both[:tall] + both[tall:]
+        index = gather_lanes(chunk + flat, places) - strip * SUBLANES
         here = lax.broadcasted_iota(jnp.int32, value.shape, 0) == index
         found = jnp.sum(jnp.where(here, value, 0.0), axis=0, keepdims=True)
         atoms = out_ref.shape[2]
@@ -271,8 +301,7 @@
     def _():
         plane_ref[...] = plane.reshape(plane_ref.shape)
         flat_ref[...] = flat.reshape(flat_ref.shape)
-        field_ref[:block, :] = field_high
-        field_ref[block:, :] = field_low
+        field_ref[:block, :], field_ref[block:, :] = split(field)
 
         def patch(p, carry):
             row, col = lax.div(p, jnp.int32(cols)), lax.rem(p, jnp.int32(cols))
@@ -441,9 +470,9 @@
     forces = pair_forces(
         positions,
         charges,
-        task_patch.reshape(-1),
-        task_near.reshape(-1),
-        task_count.reshape(-1),
+        task_patch,
+        task_near,
+        task_count,
     )
     return (forces, recip_potential)
 

time: 44.3 us -> 40.6 us (0.916)
  Pallas kernels: 15 us -> 11.3 us
    pallas_call x1, Pallas kernels: 8.65 us -> 6.01 us  [pair_forces(): pl.pallas_call(force_kernel, out_shape=jax.ShapeDtypeStruct(positions.sha...]
    pallas_call x1, Pallas kernels: 2.93 us -> 2.22 us  [spread_planes(): pl.pallas_call(spread_kernel, out_shape=pltpu.VMEM((GZ, XR * YC), jnp.flo...]
  transfers between devices with their start and end apart: 6 -> 6, of which waited for: 2 -> 2; matrix products, arithmetic and copies ran while one was open for 1% -> 1% of each run, Pallas kernels for 30% -> 25%
where the time goes in v1:
time: 40.6 us; the launch traced here: 40.2 us
  starting transfers between devices  16.4 us (40%)
  Pallas kernels  11.3 us (28%)
  waiting for transfers between devices  8.88 us (22%)
  local copies, waits for them, and re-layouts  1.84 us (5%)
  between operations  1.56 us (4%)
    all_to_all x2, starting transfers between devices, solve_planes(): held = lax.all_to_all(held, BOTH, split_axis=0, concat_axis=0, tiled=True)  11.3 us
    all_to_all x2, waiting for transfers between devices, solve_planes(): held = lax.all_to_all(held, BOTH, split_axis=0, concat_axis=0, tiled=True)  6.48 us
    pallas_call x1, Pallas kernels, pair_forces(): pl.pallas_call(force_kernel, out_shape=jax.ShapeDtypeStruct(positions.sha...  6.01 us
    ppermute x4, starting transfers between devices, from_both_sides(): return (lax.ppermute(last, axis, up), lax.ppermute(first, axis, down))  5.05 us
    ppermute x4, waiting for transfers between devices, from_both_sides(): return (lax.ppermute(last, axis, up), lax.ppermute(first, axis, down))  2.4 us
    pallas_call x1, Pallas kernels, spread_planes(): pl.pallas_call(spread_kernel, out_shape=pltpu.VMEM((GZ, XR * YC), jnp.flo...  2.22 us
    pallas_call x1, Pallas kernels, solve_planes(): pl.pallas_call(lambda *refs: xy_kernel(*refs, n_x=n_x, n_y=n_y), out_shap...  1.69 us
    pallas_call x1, Pallas kernels, sample_planes(): pl.pallas_call(sample_kernel, out_shape=jax.ShapeDtypeStruct(cells.shape,...  1.34 us
  transfers between devices with their start and end apart: 6, of which 2 were waited for; matrix products, arithmetic and copies ran while one was open for 1% of the time, Pallas kernels for 25%

profile of v1, /device:TPU:3, one launch (start us, length us, event | category | flops | bytes accessed | tf_op | source)
XLA Modules:
  0.0 40.2 jit_solution(13872679490616755216)
XLA Ops:
  0.6 0.8 %fusion.15 = (f32[8,1,128]{2,1,0:T(1,128)S(1)}, f32[8,1,128]{2,1,0:T(1,128)S(1)}) fusion(f32[8,8,128]{2,1,0:T(8,128)} %charge_hbm.1), kind=kLoop, calls=%fused_computation.40 | loop fusion | bytes 16384 | tf_op jit(solution)/shard_map/slice | solution.py:38
  1.5 0.8 %fusion.13 = (f32[1,8,8,128]{3,2,1,0:T(8,128)S(1)}, f32[1,8,8,128]{3,2,1,0:T(8,128)S(1)}, f32[1,8,8,128]{3,2,1,0:T(8,128)S(1)}) fusion(f32[3,8,8,128]{3,2,1,0:T(8,128)} %pos_ref.1), kind=kLoop, calls=%fused_computation.38 | loop fusion | bytes 196608 | tf_op jit(solution)/shard_map/unstack | solution.py:35
  2.3 0.0 copy-start.6
  2.4 0.1 collective-permute-start
  2.4 0.0 copy-start.4
  2.5 0.0 copy-start.2
  2.5 0.7 %collective-permute-start.1 = (f32[4,8,128]{2,1,0:T(8,128)S(1)}, f32[4,8,128]{2,1,0:T(8,128)S(1)}, u32[]{:S(2)}, u32[]{:S(2)}) collective-permute-start(f32[4,8,128]{2,1,0:T(8,128)S(1)} %pad_maximum_fusion.3), channel_id=1, source_target_pairs={{1,0},{2,1},{3,2},{0,3},{5,4},{6,5},{7,6},{4,7},{9,8},{10,9},{11,1... | collective-permute-start | bytes 49160 | tf_op jit(solution)/shard_map/ppermute | solution.py:31
  3.2 2.2 %spread.1 = f32[256,128]{1,0:T(8,128)} custom-call(f32[8,8,128]{2,1,0:T(8,128)} %charge_hbm.1, s32[8,8,128]{2,1,0:T(8,128)} %cell_ref.1, bf16[512,256]{1,0:T(8,128)(2,1)} %constant.49.clone.cas_hbm.cas_ref), custom_call_target="tpu_custom_call" | custom-call | tf_op jit(solution)/shard_map/spread/pallas_call | solution.py:256
  5.4 0.0 copy-start.1
  5.4 0.0 copy-start.3
  5.5 7.4 %all-to-all-start = ((f32[32,8,128]{2,1,0:T(8,128)}), f32[32,8,128]{2,1,0:T(8,128)S(1)}, u32[]{:S(2)}, u32[]{:S(2)}) async-start(f32[32,8,128]{2,1,0:T(8,128)} %bitcast.17), calls=%async_computation | async-start | bytes 262144 | tf_op jit(solution)/shard_map/all_to_all | solution.py:420
  12.9 0.0 copy-done.1
  13.0 0.1 broadcast_add_fusion
  13.1 0.1 add.57
  13.1 0.1 fusion.1.refs_1_
  13.3 0.0 copy-done.6
  13.3 0.0 collective-permute-done.1.east_ref
  13.3 6.5 %all-to-all-done.refs_0_ = f32[32,8,128]{2,1,0:T(8,128)S(1)} async-done(((f32[32,8,128]{2,1,0:T(8,128)}), f32[32,8,128]{2,1,0:T(8,128)S(1)}, u32[]{:S(2)}, u32[]{:S(2)}) %all-to-all-start) | async-done | bytes 131104 | tf_op jit(solution)/shard_map/all_to_all | solution.py:420
  19.8 0.0 copy-done.5
  19.8 0.0 copy-done.4
  19.8 1.7 %xy_solve.1 = f32[32,8,128]{2,1,0:T(8,128)} custom-call(f32[32,8,128]{2,1,0:T(8,128)S(1)} %all-to-all-done.refs_0_, f32[256,128]{1,0:T(8,128)S(1)} %fusion.1.refs_1_, bf16[512,256]{1,0:T(8,128)(2,1)S(1)} %copy-done.3, bf16[512,256]{1,0:T(8,128)(2,1)S(1)} %copy-done.4, bf16[512,256]{1,0:T(8,128)(2,1)S(1)} %copy-done.5, bf16[384,512]{1,0:T(8,128)(2,1)S(1)} %copy-done.2), custom_call_target="tpu_custom_call" | custom-call | tf_op jit(solution)/shard_map/xy_solve/pallas_call | solution.py:422
  21.5 3.9 %all-to-all-start.1 = ((f32[32,8,128]{2,1,0:T(8,128)}), f32[32,8,128]{2,1,0:T(8,128)S(1)}, u32[]{:S(2)}, u32[]{:S(2)}) async-start(f32[32,8,128]{2,1,0:T(8,128)} %xy_solve.1), calls=%async_computation.1 | async-start | bytes 262144 | tf_op jit(solution)/shard_map/all_to_all | solution.py:430
  25.4 0.0 copy-start
  25.4 0.0 collective-permute-done.west_ref
  25.5 1.3 %collective-permute-start.2 = (f32[4,10,128]{2,1,0:T(8,128)S(1)}, f32[4,10,128]{2,1,0:T(8,128)S(1)}, u32[]{:S(2)}, u32[]{:S(2)}) collective-permute-start(f32[4,10,128]{2,1,0:T(8,128)S(1)} %pad_maximum_fusion), channel_id=1, source_target_pairs={{0,4},{4,8},{8,12},{12,16},{16,20},{20,24},{24,28},{28,0},{1,5},{5... | collective-permute-start | bytes 61448 | tf_op jit(solution)/shard_map/ppermute | solution.py:31
  26.7 3.0 %collective-permute-start.3 = (f32[4,10,128]{2,1,0:T(8,128)S(1)}, f32[4,10,128]{2,1,0:T(8,128)S(1)}, u32[]{:S(2)}, u32[]{:S(2)}) collective-permute-start(f32[4,10,128]{2,1,0:T(8,128)S(1)} %pad_maximum_fusion.1), channel_id=1, source_target_pairs={{4,0},{8,4},{12,8},{16,12},{20,16},{24,20},{28,24},{0,28},{5,1},{9... | collective-permute-start | bytes 61448 | tf_op jit(solution)/shard_map/ppermute | solution.py:31
  30.4 0.0 copy-start.7
  30.4 2.4 %collective-permute-done.2.north_ref = f32[4,10,128]{2,1,0:T(8,128)S(1)} collective-permute-done((f32[4,10,128]{2,1,0:T(8,128)S(1)}, f32[4,10,128]{2,1,0:T(8,128)S(1)}, u32[]{:S(2)}, u32[]{:S(2)}) %collective-permute-start.2) | collective-permute-done | bytes 20512 | tf_op jit(solution)/shard_map/ppermute | solution.py:31
  32.8 0.0 collective-permute-done.3.south_ref
  32.8 6.0 %pair_forces.1 = f32[3,8,8,128]{3,2,1,0:T(8,128)} custom-call(s32[1,1,32]{2,1,0:T(1,128)S(1)} %copy-done.8, s32[1,1,32]{2,1,0:T(1,128)S(1)} %copy-done.9, s32[1,1]{1,0:T(1,128)S(6)} %copy.32.count_ref, f32[3,8,8,128]{3,2,1,0:T(8,128)S(1)} %copy-done.1, f32[8,8,128]{2,1,0:T(8,128)S(1)} %copy-done.6, f32[4,8,128]{2,1,0:T(8,128)S(1)} %collective-permute-done.west_ref, ...), custom_call_target="tpu_custom_call" | custom-call | tf_op jit(solution)/shard_map/pair_forces/pallas_call | solution.py:138
  38.8 0.0 all-to-all-done.1
  38.8 1.3 %sample.1 = f32[8,8,128]{2,1,0:T(8,128)} custom-call(f32[256,128]{1,0:T(8,128)S(1)} %bitcast.39, s32[8,8,128]{2,1,0:T(8,128)S(1)} %copy-done.7, bf16[512,256]{1,0:T(8,128)(2,1)S(1)} %copy-done), custom_call_target="tpu_custom_call" | custom-call | tf_op jit(solution)/shard_map/sample/pallas_call | solution.py:322
  (25 shorter events, 0.1 us)
Async XLA Ops:
  2.3 17.5 %copy-start.5 = (bf16[512,256]{1,0:T(8,128)(2,1)S(1)}, bf16[512,256]{1,0:T(8,128)(2,1)}, u32[]{:S(2)}) copy-start(bf16[512,256]{1,0:T(8,128)(2,1)} %constant.52.clone.refs_4_) | copy-start | bytes 786436
  2.3 10.9 %copy-start.6 = (f32[8,8,128]{2,1,0:T(8,128)S(1)}, f32[8,8,128]{2,1,0:T(8,128)}, u32[]{:S(2)}) copy-start(f32[8,8,128]{2,1,0:T(8,128)} %charge_hbm.1) | copy-start | bytes 98308
  2.4 23.0 %collective-permute-start = (f32[4,8,128]{2,1,0:T(8,128)S(1)}, f32[4,8,128]{2,1,0:T(8,128)S(1)}, u32[]{:S(2)}, u32[]{:S(2)}) collective-permute-start(f32[4,8,128]{2,1,0:T(8,128)S(1)} %pad_maximum_fusion.2), channel_id=1, source_target_pairs={{0,1},{1,2},{2,3},{3,0},{4,5},{5,6},{6,7},{7,4},{8,9},{9,10},{10,1... | collective-permute-start | bytes 49160 | tf_op jit(solution)/shard_map/ppermute | solution.py:31
  2.4 17.4 %copy-start.4 = (bf16[512,256]{1,0:T(8,128)(2,1)S(1)}, bf16[512,256]{1,0:T(8,128)(2,1)}, u32[]{:S(2)}) copy-start(bf16[512,256]{1,0:T(8,128)(2,1)} %constant.51.clone.refs_3_) | copy-start | bytes 786436
  2.5 17.3 %copy-start.2 = (bf16[384,512]{1,0:T(8,128)(2,1)S(1)}, bf16[384,512]{1,0:T(8,128)(2,1)}, u32[]{:S(2)}) copy-start(bf16[384,512]{1,0:T(8,128)(2,1)} %constant.53.clone.refs_5_) | copy-start | bytes 1179652
  2.5 10.8 %collective-permute-start.1 = (f32[4,8,128]{2,1,0:T(8,128)S(1)}, f32[4,8,128]{2,1,0:T(8,128)S(1)}, u32[]{:S(2)}, u32[]{:S(2)}) collective-permute-start(f32[4,8,128]{2,1,0:T(8,128)S(1)} %pad_maximum_fusion.3), channel_id=1, source_target_pairs={{1,0},{2,1},{3,2},{0,3},{5,4},{6,5},{7,6},{4,7},{9,8},{10,9},{11,1... | collective-permute-start | bytes 49160 | tf_op jit(solution)/shard_map/ppermute | solution.py:31
  5.4 7.5 %copy-start.1 = (f32[3,8,8,128]{3,2,1,0:T(8,128)S(1)}, f32[3,8,8,128]{3,2,1,0:T(8,128)}, u32[]{:S(2)}) copy-start(f32[3,8,8,128]{3,2,1,0:T(8,128)} %pos_ref.1) | copy-start | bytes 294916
  5.4 14.4 %copy-start.3 = (bf16[512,256]{1,0:T(8,128)(2,1)S(1)}, bf16[512,256]{1,0:T(8,128)(2,1)}, u32[]{:S(2)}) copy-start(bf16[512,256]{1,0:T(8,128)(2,1)} %constant.50.clone.refs_2_) | copy-start | bytes 786436
  5.5 14.3 %all-to-all-start = ((f32[32,8,128]{2,1,0:T(8,128)}), f32[32,8,128]{2,1,0:T(8,128)S(1)}, u32[]{:S(2)}, u32[]{:S(2)}) async-start(f32[32,8,128]{2,1,0:T(8,128)} %bitcast.17), calls=%async_computation | async-start | bytes 262144 | tf_op jit(solution)/shard_map/all_to_all | solution.py:420
  21.5 11.3 %copy-start.8 = (s32[1,1,32]{2,1,0:T(1,128)S(1)}, s32[1,1,32]{2,1,0:T(1,128)}, u32[]{:S(2)}) copy-start(s32[1,1,32]{2,1,0:T(1,128)} %patch_ref.1) | copy-start | bytes 388
  21.5 11.3 %copy-start.9 = (s32[1,1,32]{2,1,0:T(1,128)S(1)}, s32[1,1,32]{2,1,0:T(1,128)}, u32[]{:S(2)}) copy-start(s32[1,1,32]{2,1,0:T(1,128)} %near_ref.1) | copy-start | bytes 388
  21.5 17.3 %all-to-all-start.1 = ((f32[32,8,128]{2,1,0:T(8,128)}), f32[32,8,128]{2,1,0:T(8,128)S(1)}, u32[]{:S(2)}, u32[]{:S(2)}) async-start(f32[32,8,128]{2,1,0:T(8,128)} %xy_solve.1), calls=%async_computation.1 | async-start | bytes 262144 | tf_op jit(solution)/shard_map/all_to_all | solution.py:430
  25.4 13.4 %copy-start = (bf16[512,256]{1,0:T(8,128)(2,1)S(1)}, bf16[512,256]{1,0:T(8,128)(2,1)}, u32[]{:S(2)}) copy-start(bf16[512,256]{1,0:T(8,128)(2,1)} %constant.49.clone.cas_hbm.cas_ref) | copy-start | bytes 786436
  25.5 7.3 %collective-permute-start.2 = (f32[4,10,128]{2,1,0:T(8,128)S(1)}, f32[4,10,128]{2,1,0:T(8,128)S(1)}, u32[]{:S(2)}, u32[]{:S(2)}) collective-permute-start(f32[4,10,128]{2,1,0:T(8,128)S(1)} %pad_maximum_fusion), channel_id=1, source_target_pairs={{0,4},{4,8},{8,12},{12,16},{16,20},{20,24},{24,28},{28,0},{1,5},{5... | collective-permute-start | bytes 61448 | tf_op jit(solution)/shard_map/ppermute | solution.py:31
  26.7 6.1 %collective-permute-start.3 = (f32[4,10,128]{2,1,0:T(8,128)S(1)}, f32[4,10,128]{2,1,0:T(8,128)S(1)}, u32[]{:S(2)}, u32[]{:S(2)}) collective-permute-start(f32[4,10,128]{2,1,0:T(8,128)S(1)} %pad_maximum_fusion.1), channel_id=1, source_target_pairs={{4,0},{8,4},{12,8},{16,12},{20,16},{24,20},{28,24},{0,28},{5,1},{9... | collective-permute-start | bytes 61448 | tf_op jit(solution)/shard_map/ppermute | solution.py:31
  30.4 8.4 %copy-start.7 = (s32[8,8,128]{2,1,0:T(8,128)S(1)}, s32[8,8,128]{2,1,0:T(8,128)}, u32[]{:S(2)}) copy-start(s32[8,8,128]{2,1,0:T(8,128)} %cell_ref.1) | copy-start | bytes 98308
